TPU v7x, 128 devices: a whole 4x4x4 slice. The times are simulated.
128 devices in a mesh: subset: 8 (over y, z_lo), tile: 16 (over z_hi, x, core).
Axes of the slice: x: 4, y: 4, z: 4 (z_hi: 2, z_lo: 2; z = z_hi * 2 + z_lo), core: 2. Of those that a mesh axis runs over, the one named last changes fastest.
Arguments:
- start_volume: bfloat16 [8, 64, 65536], P(None, None, 'tile'), may hold values from 0 to 2
- measured: bfloat16 [8, 8, 64, 2048], P('subset'), may hold values from 6528 to 26112
- system_values: bfloat16 [8, 2048, 65536], P('subset', None, 'tile'), may hold values from 0.05 to 2088.96, as said below
- block_pattern: int32 [8, 16, 512], P('subset', None, 'tile'), may hold values from 0 to 1, as said below
- subset_order: int32 [64, 8], replicated, may hold values from 0 to 7, each once within a row
Outputs:
- volume_out: bfloat16 [8, 64, 65536], P(None, None, 'tile')
Inputs may be any that keep to these rules, and one draw needn't show every extreme that they name: `block_pattern`: each entry is 0 or 1; every block row and every block column of each subset's matrix within every 4096-voxel tile holds at least one 1. `system_values`: positive entries. `subset_order`: each row is a permutation of the 8 subsets.
All inputs are finite; a program needn't handle non-finite values.
Results may differ from a plain program's by a relative error of at most 0.0034.
Values may be sent and summed in bfloat16 or wider, within the bound.
A program may use at most 128 MiB of HBM per device.

v0:
```python
import jax
import jax.numpy as jnp
from jax import lax
from jax.sharding import PartitionSpec as P

BLOCK_SIDE = 128
SWEEP_PASSES = 4


def passed_along(block, axis, distance):
    devices = range(lax.axis_size(axis))
    route = [((i - distance) % len(devices), i) for i in devices]
    return lax.ppermute(block, axis, route)


def body(start_volume, measured, system_values, block_pattern, subset_order):
    owner_idx = lax.axis_index("subset")
    holder_count = lax.axis_size("subset")
    pattern = block_pattern[0].astype(jnp.bfloat16)
    matrix = system_values[0] * jnp.repeat(jnp.repeat(pattern, BLOCK_SIDE, 0), BLOCK_SIDE, 1)
    column_sum = jnp.sum(matrix, axis=0, dtype=jnp.float32)
    row_part = jnp.sum(matrix, axis=1, dtype=jnp.float32)[None, :]
    slice_measurement = measured[0]

    def subset_selector(slice_portion):
        source = (owner_idx - slice_portion) % holder_count
        return (subset_order == source).astype(jnp.bfloat16)

    volume = jnp.einsum(
        "sf,fsv->sv", subset_selector(0), start_volume, preferred_element_type=jnp.float32
    )
    ray_total = lax.psum(row_part, "tile")
    for slice_portion in range(SWEEP_PASSES):
        selected_subset = subset_selector(slice_portion)
        destination_rows = jnp.einsum(
            "ej,jev->ev", selected_subset, slice_measurement, preferred_element_type=jnp.float32
        )
        narrow = volume.astype(jnp.bfloat16)
        partial_value = lax.dot_general(
            narrow, matrix, (((1,), (1,)), ((), ())), preferred_element_type=jnp.float32
        )
        projected = lax.psum(partial_value, "tile")
        residue = ((destination_rows - projected) / ray_total).astype(jnp.bfloat16)
        spread_back = jnp.dot(residue, matrix, preferred_element_type=jnp.float32)
        volume = volume + spread_back / column_sum[None, :]
        if slice_portion + 1 < SWEEP_PASSES:
            volume = passed_along(volume, "subset", 1)
    final_pick = subset_selector(SWEEP_PASSES - 1).astype(jnp.float32)
    rounded = lax.optimization_barrier(volume.astype(jnp.bfloat16)).astype(jnp.float32)
    contribution = jnp.transpose(final_pick)[:, :, None] * rounded[None, :, :]
    gathered = lax.psum(contribution.astype(jnp.bfloat16), "subset")
    return gathered


def solution(mesh):
    placed = (
        P(None, None, "tile"),
        P("subset", None, None, None),
        P("subset", None, "tile"),
        P("subset", None, "tile"),
        P(),
    )
    return jax.shard_map(
        body, mesh=mesh, in_specs=placed, out_specs=P(None, None, "tile"), check_vma=False
    )
```

profile of v0, /device:TPU:16, one launch (start us, length us, event | category | flops | bytes accessed | tf_op | source)
XLA Modules:
  0.0 966.0 jit_solution(6587851373304264414)
XLA Ops:
  8.3 25.4 %broadcast_in_dim.7 = bf16[2048,32,128]{2,1,0:T(8,128)(2,1)S(1)} broadcast(bf16[2048,32]{1,0:T(8,128)(2,1)S(1)} %bitcast.70), dimensions={0,1} | broadcast | bytes 16908288 | tf_op jit(solution)/shard_map/broadcast_in_dim | solution.py:20
  33.7 14.5 %convert_reduce_fusion.1 = (f32[2048]{0:T(1024)S(1)}, f32[4096]{0:T(1024)S(1)}, bf16[2048,4096]{1,0:T(8,128)(2,1)}) fusion(bf16[256,8,32,128]{3,2,1,0:T(8,128)(2,1)S(1)} %bitcast.69, bf16[1,2048,4096]{2,1,0:T(8,128)(2,1)} %param.7), kind=kLoop, calls=%fused_computation.1 | loop fusion | flops 33548288 | bytes 50356224 | tf_op jit(solution)/shard_map/reduce_sum | solution.py:22
  48.2 5.0 fusion.5
  53.2 11.8 %fusion.15 = f32[64,2048]{1,0:T(8,128)} fusion(bf16[2048,4096]{1,0:T(8,128)(2,1)} %get-tuple-element.9, f32[64,1,4096]{2,1,0:T(1,128)S(1)} %fusion.5), kind=kOutput, calls=%fused_computation.24 | convolution fusion | flops 1073741824 | bytes 18350080 | tf_op jit(solution)/shard_map/dot_general | solution.py:39
  65.6 39.2 %psum.43 = f32[2048]{0:T(1024)S(1)} all-reduce(f32[2048]{0:T(1024)S(1)} %get-tuple-element.5), channel_id=1, replica_groups=mesh['subset'=8,'tile'=16] {'tile'}, use_global_device_ids=true, to_apply=%region_2.3 | all-reduce | flops 2048 | bytes 16384 | tf_op jit(solution)/shard_map/psum | solution.py:32
  107.1 100.0 %all-reduce.6.cloned.1.call-done = f32[64,2048]{1,0:T(8,128)} async-done(((f32[64,2048]{1,0:T(8,128)}), f32[64,2048]{1,0:T(8,128)}) %all-reduce.6.cloned.1.call-update) | async-done | bytes 524304 | tf_op jit(solution)/shard_map/psum | solution.py:42
  207.1 9.6 fusion.3
  218.0 24.7 %collective-permute-done = f32[64,4096]{1,0:T(8,128)S(1)} collective-permute-done((f32[64,4096]{1,0:T(8,128)S(1)}, f32[64,4096]{1,0:T(8,128)S(1)}, u32[]{:S(2)}, u32[]{:S(2)}) %collective-permute-start) | collective-permute-done | bytes 1048608 | tf_op jit(solution)/shard_map/ppermute | solution.py:13
  242.6 11.7 %fusion.28 = f32[64,2048]{1,0:T(8,128)} fusion(bf16[2048,4096]{1,0:T(8,128)(2,1)} %get-tuple-element.9, f32[64,4096]{1,0:T(8,128)S(1)} %collective-permute-done), kind=kOutput, calls=%fused_computation.41 | convolution fusion | flops 1074003968 | bytes 18350080 | tf_op jit(solution)/shard_map/dot_general | solution.py:39
  257.1 133.7 %all-reduce.8.cloned.1.call-done = f32[64,2048]{1,0:T(8,128)} async-done(((f32[64,2048]{1,0:T(8,128)}), f32[64,2048]{1,0:T(8,128)}) %all-reduce.8.cloned.1.call-update) | async-done | bytes 524304 | tf_op jit(solution)/shard_map/psum | solution.py:42
  390.8 9.2 fusion.2
  401.1 24.7 %collective-permute-done.1 = f32[64,4096]{1,0:T(8,128)S(1)} collective-permute-done((f32[64,4096]{1,0:T(8,128)S(1)}, f32[64,4096]{1,0:T(8,128)S(1)}, u32[]{:S(2)}, u32[]{:S(2)}) %collective-permute-start.1) | collective-permute-done | bytes 1048608 | tf_op jit(solution)/shard_map/ppermute | solution.py:13
  425.8 11.7 %fusion.26 = f32[64,2048]{1,0:T(8,128)} fusion(bf16[2048,4096]{1,0:T(8,128)(2,1)} %get-tuple-element.9, f32[64,4096]{1,0:T(8,128)S(1)} %collective-permute-done.1), kind=kOutput, calls=%fused_computation.39 | convolution fusion | flops 1074003968 | bytes 18350080 | tf_op jit(solution)/shard_map/dot_general | solution.py:39
  437.7 2.4 fusion.9
  440.1 133.9 %all-reduce.10.cloned.1.call-done = f32[64,2048]{1,0:T(8,128)} async-done(((f32[64,2048]{1,0:T(8,128)}), f32[64,2048]{1,0:T(8,128)}) %all-reduce.10.cloned.1.call-update) | async-done | bytes 524304 | tf_op jit(solution)/shard_map/psum | solution.py:42
  573.9 9.2 fusion.1
  584.5 24.7 %collective-permute-done.2 = f32[64,4096]{1,0:T(8,128)S(1)} collective-permute-done((f32[64,4096]{1,0:T(8,128)S(1)}, f32[64,4096]{1,0:T(8,128)S(1)}, u32[]{:S(2)}, u32[]{:S(2)}) %collective-permute-start.2) | collective-permute-done | bytes 1048608 | tf_op jit(solution)/shard_map/ppermute | solution.py:13
  609.2 11.7 %fusion.24 = f32[64,2048]{1,0:T(8,128)} fusion(bf16[2048,4096]{1,0:T(8,128)(2,1)} %get-tuple-element.9, f32[64,4096]{1,0:T(8,128)S(1)} %collective-permute-done.2), kind=kOutput, calls=%fused_computation.37 | convolution fusion | flops 1074003968 | bytes 18350080 | tf_op jit(solution)/shard_map/dot_general | solution.py:39
  621.1 2.4 fusion.7
  623.5 133.9 %all-reduce.12.cloned.1.call-done = f32[64,2048]{1,0:T(8,128)} async-done(((f32[64,2048]{1,0:T(8,128)}), f32[64,2048]{1,0:T(8,128)}) %all-reduce.12.cloned.1.call-update) | async-done | bytes 524304 | tf_op jit(solution)/shard_map/psum | solution.py:42
  757.3 9.2 fusion.4
  766.6 3.1 multiply_convert_fusion
  769.7 184.8 %all-reduce.14.cloned.1.call-done = bf16[8,64,4096]{2,1,0:T(8,128)(2,1)} async-done(((bf16[8,64,4096]{2,1,0:T(8,128)(2,1)}), bf16[8,64,4096]{2,1,0:T(8,128)(2,1)}) %all-reduce.14.cloned.1.call-update) | async-done | bytes 4194320 | tf_op jit(solution)/shard_map/psum | solution.py:51
  954.5 4.7 copy.46
  (27 shorter events, 11.6 us)
Async XLA Ops:
  6.5 98.2 %copy-start = (bf16[1,8,64,2048]{3,2,1,0:T(8,128)(2,1)S(1)}, bf16[1,8,64,2048]{3,2,1,0:T(8,128)(2,1)}, u32[]{:S(2)}) copy-start(bf16[1,8,64,2048]{3,2,1,0:T(8,128)(2,1)} %param.6) | copy-start | bytes 6291460
  6.5 200.6 %all-reduce.6.cloned.1.call-start = ((), (), s32[]{:S(2)}) async-start(), calls=%async_computation | async-start | bytes 1048576 | tf_op jit(solution)/shard_map/psum | solution.py:42
  33.7 14.5 %copy-start.1 = (bf16[8,64,4096]{2,1,0:T(8,128)(2,1)S(1)}, bf16[8,64,4096]{2,1,0:T(8,128)(2,1)}, u32[]{:S(2)}) copy-start(bf16[8,64,4096]{2,1,0:T(8,128)(2,1)} %param.5) | copy-start | bytes 12582916
  65.1 325.7 %all-reduce.8.cloned.1.call-start = ((), (), s32[]{:S(2)}) async-start(), calls=%async_computation.1 | async-start | bytes 1048576 | tf_op jit(solution)/shard_map/psum | solution.py:42
  216.7 25.9 %collective-permute-start = (f32[64,4096]{1,0:T(8,128)S(1)}, f32[64,4096]{1,0:T(8,128)S(1)}, u32[]{:S(2)}, u32[]{:S(2)}) collective-permute-start(f32[64,4096]{1,0:T(8,128)S(1)} %fusion.3), channel_id=1, source_target_pairs={{112,0},{0,16},{16,32},{32,48},{48,64},{64,80},{80,96},{96,112},{1... | collective-permute-start | bytes 3145736 | tf_op jit(solution)/shard_map/ppermute | solution.py:13
  254.4 319.6 %all-reduce.10.cloned.1.call-start = ((), (), s32[]{:S(2)}) async-start(), calls=%async_computation.2 | async-start | bytes 1048576 | tf_op jit(solution)/shard_map/psum | solution.py:42
  399.9 25.9 %collective-permute-start.1 = (f32[64,4096]{1,0:T(8,128)S(1)}, f32[64,4096]{1,0:T(8,128)S(1)}, u32[]{:S(2)}, u32[]{:S(2)}) collective-permute-start(f32[64,4096]{1,0:T(8,128)S(1)} %fusion.2), channel_id=1, source_target_pairs={{112,0},{0,16},{16,32},{32,48},{48,64},{64,80},{80,96},{96,112},{1... | collective-permute-start | bytes 3145736 | tf_op jit(solution)/shard_map/ppermute | solution.py:13
  437.5 319.8 %all-reduce.12.cloned.1.call-start = ((), (), s32[]{:S(2)}) async-start(), calls=%async_computation.3 | async-start | bytes 1048576 | tf_op jit(solution)/shard_map/psum | solution.py:42
  583.1 26.1 %collective-permute-start.2 = (f32[64,4096]{1,0:T(8,128)S(1)}, f32[64,4096]{1,0:T(8,128)S(1)}, u32[]{:S(2)}, u32[]{:S(2)}) collective-permute-start(f32[64,4096]{1,0:T(8,128)S(1)} %fusion.1), channel_id=1, source_target_pairs={{112,0},{0,16},{16,32},{32,48},{48,64},{64,80},{80,96},{96,112},{1... | collective-permute-start | bytes 3145736 | tf_op jit(solution)/shard_map/ppermute | solution.py:13
  620.9 333.6 %all-reduce.14.cloned.1.call-start = ((), (), s32[]{:S(2)}) async-start(), calls=%async_computation.4 | async-start | bytes 8388608 | tf_op jit(solution)/shard_map/psum | solution.py:51
Sparse Core Ops, SparseCore 0:
  65.2 141.8 all-reduce.5
  254.5 136.2 all-reduce.7
  437.7 136.2 all-reduce.9
  621.1 136.2 all-reduce.11
  769.8 184.6 all-reduce.13
where the time goes:
time: 975 us; the launch traced here: 966 us
  waiting for transfers between devices  760 us (78%)
  matrix products  98.5 us (10%)
  blocking collectives  39.2 us (4%)
  local copies, waits for them, and re-layouts  30.7 us (3%)
  other arithmetic  19.2 us (2%)
  between operations  13.4 us (1%)
    psum x4, waiting for transfers between devices, body(): projected = lax.psum(partial_value, 'tile')  501 us
    psum x1, waiting for transfers between devices, body(): gathered = lax.psum(contribution.astype(jnp.bfloat16), 'subset')  185 us
    ppermute x3, waiting for transfers between devices, passed_along(): return lax.ppermute(block, axis, route)  74 us
    dot_general x4, matrix products, body(): lax.dot_general(narrow, matrix, (((1,), (1,)), ((), ())), preferred_eleme...  47.1 us
    psum x1, blocking collectives, body(): ray_total = lax.psum(row_part, 'tile')  39.2 us
    dot_general x4, matrix products, body(): spread_back = jnp.dot(residue, matrix, preferred_element_type=jnp.float32)  37.1 us
    broadcast_in_dim x1, local copies, waits for them, and re-layouts, body(): jnp.repeat(jnp.repeat(pattern, BLOCK_SIDE, 0), BLOCK_SIDE, 1)  25.4 us
  transfers between devices with their start and end apart: 8, of which 8 were waited for; matrix products, arithmetic and copies ran while one was open for 1% of the time, Pallas kernels for 0%

commit v1 on v0

--- a/solution.py
+++ b/solution.py
@@ -5,6 +5,12 @@
 
 BLOCK_SIDE = 128
 SWEEP_PASSES = 4
+
+
+def add_all(x, axis):
+    pieces = lax.all_gather(x, axis, axis=0, tiled=False)
+    total = pieces.sum(axis=0)
+    return total
 
 
 def passed_along(block, axis, distance):
@@ -39,7 +45,7 @@
         partial_value = lax.dot_general(
             narrow, matrix, (((1,), (1,)), ((), ())), preferred_element_type=jnp.float32
         )
-        projected = lax.psum(partial_value, "tile")
+        projected = add_all(partial_value, "tile")
         residue = ((destination_rows - projected) / ray_total).astype(jnp.bfloat16)
         spread_back = jnp.dot(residue, matrix, preferred_element_type=jnp.float32)
         volume = volume + spread_back / column_sum[None, :]

time: 975 us -> 725 us (0.74)
  waiting for transfers between devices: 760 us -> 493 us
  other arithmetic: 19.2 us -> 38.2 us
    psum x4 -> x0, waiting for transfers between devices: 501 us -> none  [body(): projected = lax.psum(partial_value, 'tile')]
    all_gather x0 -> x4, waiting for transfers between devices: none -> 235 us  [add_all(): pieces = lax.all_gather(x, axis, axis=0, tiled=False)]
    reduce_sum x0 -> x4, other arithmetic: none -> 18.9 us  [add_all(): total = pieces.sum(axis=0)]
where the time goes in v1:
time: 725 us; the launch traced here: 717 us
  waiting for transfers between devices  493 us (68%)
  matrix products  98.7 us (14%)
  blocking collectives  39.3 us (5%)
  other arithmetic  38.2 us (5%)
  local copies, waits for them, and re-layouts  30.7 us (4%)
  between operations  13.5 us (2%)
    all_gather x4, waiting for transfers between devices, add_all(): pieces = lax.all_gather(x, axis, axis=0, tiled=False)  235 us
    psum x1, waiting for transfers between devices, body(): gathered = lax.psum(contribution.astype(jnp.bfloat16), 'subset')  181 us
    ppermute x3, waiting for transfers between devices, passed_along(): return lax.ppermute(block, axis, route)  76.6 us
    dot_general x4, matrix products, body(): lax.dot_general(narrow, matrix, (((1,), (1,)), ((), ())), preferred_eleme...  47.1 us
    psum x1, blocking collectives, body(): ray_total = lax.psum(row_part, 'tile')  39.3 us
    dot_general x4, matrix products, body(): spread_back = jnp.dot(residue, matrix, preferred_element_type=jnp.float32)  37.1 us
    broadcast_in_dim x1, local copies, waits for them, and re-layouts, body(): jnp.repeat(jnp.repeat(pattern, BLOCK_SIDE, 0), BLOCK_SIDE, 1)  25.4 us
    reduce_sum x4, other arithmetic, add_all(): total = pieces.sum(axis=0)  18.9 us
  transfers between devices with their start and end apart: 8, of which 8 were waited for; matrix products, arithmetic and copies ran while one was open for 1% of the time, Pallas kernels for 0%

profile of v1, /device:TPU:16, one launch (start us, length us, event | category | flops | bytes accessed | tf_op | source)
XLA Modules:
  0.0 716.6 jit_solution(11204942570828800561)
XLA Ops:
  8.3 25.4 %broadcast_in_dim.7 = bf16[2048,32,128]{2,1,0:T(8,128)(2,1)S(1)} broadcast(bf16[2048,32]{1,0:T(8,128)(2,1)S(1)} %bitcast.78), dimensions={0,1} | broadcast | bytes 16908288 | tf_op jit(solution)/shard_map/broadcast_in_dim | solution.py:26
  33.7 14.5 %convert_reduce_fusion.1 = (f32[2048]{0:T(1024)S(1)}, f32[4096]{0:T(1024)S(1)}, bf16[2048,4096]{1,0:T(8,128)(2,1)}) fusion(bf16[256,8,32,128]{3,2,1,0:T(8,128)(2,1)S(1)} %bitcast.73, bf16[1,2048,4096]{2,1,0:T(8,128)(2,1)} %param.7), kind=kLoop, calls=%fused_computation.1 | loop fusion | flops 33548288 | bytes 50356224 | tf_op jit(solution)/shard_map/reduce_sum | solution.py:28
  48.2 5.0 fusion.5
  53.2 11.8 %fusion.15 = f32[64,2048]{1,0:T(8,128)} fusion(bf16[2048,4096]{1,0:T(8,128)(2,1)} %get-tuple-element.9, f32[64,1,4096]{2,1,0:T(1,128)S(1)} %fusion.5), kind=kOutput, calls=%fused_computation.24 | convolution fusion | flops 1073741824 | bytes 18350080 | tf_op jit(solution)/shard_map/dot_general | solution.py:45
  65.7 39.3 %psum.14 = f32[2048]{0:T(1024)S(1)} all-reduce(f32[2048]{0:T(1024)S(1)} %get-tuple-element.5), channel_id=1, replica_groups=mesh['subset'=8,'tile'=16] {'tile'}, use_global_device_ids=true, to_apply=%region_2.3 | all-reduce | flops 2048 | bytes 16384 | tf_op jit(solution)/shard_map/psum | solution.py:38
  107.3 32.9 %all-gather.9.cloned.1.call-done = f32[1024,2048]{1,0:T(8,128)} async-done(((f32[64,2048]{1,0:T(8,128)}), f32[1024,2048]{1,0:T(8,128)}) %all-gather.9.cloned.1.call-update) | async-done | bytes 8388624 | tf_op jit(solution)/shard_map/all_gather | solution.py:11
  140.2 4.7 reduce_sum.54
  144.9 9.6 %fusion.3 = f32[64,4096]{1,0:T(8,128)S(1)} fusion(bf16[2048,4096]{1,0:T(8,128)(2,1)} %get-tuple-element.9, f32[64,1,4096]{2,1,0:T(1,128)S(1)} %fusion.5, f32[4096]{0:T(1024)S(1)} %get-tuple-element.6, f32[64,2048]{1,0:T(8,128)} %reduce_sum.54, f32[64,1,2048]{2,1,0:T(1,128)} %fusion.13, f32[2048]{0:T(1024)S(1)} %psum.14), kind=kOutput, calls=%fused_computation.11 | convolution fusion | flops 1074659328 | bytes 19947520 | tf_op jit(solution)/shard_map/dot_general | solution.py:50
  155.3 25.5 %collective-permute-done = f32[64,4096]{1,0:T(8,128)S(1)} collective-permute-done((f32[64,4096]{1,0:T(8,128)S(1)}, f32[64,4096]{1,0:T(8,128)S(1)}, u32[]{:S(2)}, u32[]{:S(2)}) %collective-permute-start) | collective-permute-done | bytes 1048608 | tf_op jit(solution)/shard_map/ppermute | solution.py:19
  180.8 11.7 %fusion.28 = f32[64,2048]{1,0:T(8,128)} fusion(bf16[2048,4096]{1,0:T(8,128)(2,1)} %get-tuple-element.9, f32[64,4096]{1,0:T(8,128)S(1)} %collective-permute-done), kind=kOutput, calls=%fused_computation.41 | convolution fusion | flops 1074003968 | bytes 18350080 | tf_op jit(solution)/shard_map/dot_general | solution.py:45
  195.3 67.3 %all-gather.11.cloned.1.call-done = f32[1024,2048]{1,0:T(8,128)} async-done(((f32[64,2048]{1,0:T(8,128)}), f32[1024,2048]{1,0:T(8,128)}) %all-gather.11.cloned.1.call-update) | async-done | bytes 8388624 | tf_op jit(solution)/shard_map/all_gather | solution.py:11
  262.7 4.7 reduce_sum.57
  267.4 9.2 %fusion.2 = f32[64,4096]{1,0:T(8,128)S(1)} fusion(f32[64,4096]{1,0:T(8,128)S(1)} %collective-permute-done, bf16[2048,4096]{1,0:T(8,128)(2,1)} %get-tuple-element.9, f32[4096]{0:T(1024)S(1)} %get-tuple-element.6, f32[64,2048]{1,0:T(8,128)} %reduce_sum.57, f32[64,1,2048]{2,1,0:T(1,128)} %fusion.11, f32[2048]{0:T(1024)S(1)} %psum.14), kind=kOutput, calls=%fused_computation.9 | convolution fusion | flops 1074659328 | bytes 19947520 | tf_op jit(solution)/shard_map/dot_general | solution.py:50
  277.3 25.5 %collective-permute-done.1 = f32[64,4096]{1,0:T(8,128)S(1)} collective-permute-done((f32[64,4096]{1,0:T(8,128)S(1)}, f32[64,4096]{1,0:T(8,128)S(1)}, u32[]{:S(2)}, u32[]{:S(2)}) %collective-permute-start.1) | collective-permute-done | bytes 1048608 | tf_op jit(solution)/shard_map/ppermute | solution.py:19
  302.8 11.7 %fusion.26 = f32[64,2048]{1,0:T(8,128)} fusion(bf16[2048,4096]{1,0:T(8,128)(2,1)} %get-tuple-element.9, f32[64,4096]{1,0:T(8,128)S(1)} %collective-permute-done.1), kind=kOutput, calls=%fused_computation.39 | convolution fusion | flops 1074003968 | bytes 18350080 | tf_op jit(solution)/shard_map/dot_general | solution.py:45
  317.4 67.3 %all-gather.13.cloned.1.call-done = f32[1024,2048]{1,0:T(8,128)} async-done(((f32[64,2048]{1,0:T(8,128)}), f32[1024,2048]{1,0:T(8,128)}) %all-gather.13.cloned.1.call-update) | async-done | bytes 8388624 | tf_op jit(solution)/shard_map/all_gather | solution.py:11
  384.6 4.7 reduce_sum.58
  389.4 9.2 %fusion.1 = f32[64,4096]{1,0:T(8,128)S(1)} fusion(f32[64,4096]{1,0:T(8,128)S(1)} %collective-permute-done.1, bf16[2048,4096]{1,0:T(8,128)(2,1)} %get-tuple-element.9, f32[4096]{0:T(1024)S(1)} %get-tuple-element.6, f32[64,2048]{1,0:T(8,128)} %reduce_sum.58, f32[64,1,2048]{2,1,0:T(1,128)} %fusion.9, f32[2048]{0:T(1024)S(1)} %psum.14), kind=kOutput, calls=%fused_computation.7 | convolution fusion | flops 1074659328 | bytes 19947520 | tf_op jit(solution)/shard_map/dot_general | solution.py:50
  399.2 25.5 %collective-permute-done.2 = f32[64,4096]{1,0:T(8,128)S(1)} collective-permute-done((f32[64,4096]{1,0:T(8,128)S(1)}, f32[64,4096]{1,0:T(8,128)S(1)}, u32[]{:S(2)}, u32[]{:S(2)}) %collective-permute-start.2) | collective-permute-done | bytes 1048608 | tf_op jit(solution)/shard_map/ppermute | solution.py:19
  424.8 11.7 %fusion.24 = f32[64,2048]{1,0:T(8,128)} fusion(bf16[2048,4096]{1,0:T(8,128)(2,1)} %get-tuple-element.9, f32[64,4096]{1,0:T(8,128)S(1)} %collective-permute-done.2), kind=kOutput, calls=%fused_computation.37 | convolution fusion | flops 1074003968 | bytes 18350080 | tf_op jit(solution)/shard_map/dot_general | solution.py:45
  439.4 67.2 %all-gather.15.cloned.1.call-done = f32[1024,2048]{1,0:T(8,128)} async-done(((f32[64,2048]{1,0:T(8,128)}), f32[1024,2048]{1,0:T(8,128)}) %all-gather.15.cloned.1.call-update) | async-done | bytes 8388624 | tf_op jit(solution)/shard_map/all_gather | solution.py:11
  506.6 4.7 reduce_sum.59
  511.3 9.2 %fusion.4 = bf16[64,4096]{1,0:T(8,128)(2,1)S(1)} fusion(f32[64,4096]{1,0:T(8,128)S(1)} %collective-permute-done.2, bf16[2048,4096]{1,0:T(8,128)(2,1)} %get-tuple-element.9, f32[4096]{0:T(1024)S(1)} %get-tuple-element.6, f32[64,2048]{1,0:T(8,128)} %reduce_sum.59, f32[64,1,2048]{2,1,0:T(1,128)} %fusion.7, f32[2048]{0:T(1024)S(1)} %psum.14), kind=kOutput, calls=%fused_computation.12 | convolution fusion | flops 1074921472 | bytes 19423232 | tf_op jit(solution)/shard_map/dot_general | solution.py:50
  523.7 181.4 %all-reduce.2.cloned.1.call-done = bf16[8,64,4096]{2,1,0:T(8,128)(2,1)} async-done(((bf16[8,64,4096]{2,1,0:T(8,128)(2,1)}), bf16[8,64,4096]{2,1,0:T(8,128)(2,1)}) %all-reduce.2.cloned.1.call-update) | async-done | bytes 4194320 | tf_op jit(solution)/shard_map/psum | solution.py:57
  (31 shorter events, 23.1 us)
Async XLA Ops:
  6.5 98.4 %copy-start = (bf16[1,8,64,2048]{3,2,1,0:T(8,128)(2,1)S(1)}, bf16[1,8,64,2048]{3,2,1,0:T(8,128)(2,1)}, u32[]{:S(2)}) copy-start(bf16[1,8,64,2048]{3,2,1,0:T(8,128)(2,1)} %param.6) | copy-start | bytes 6291460
  6.5 133.7 %all-gather.9.cloned.1.call-start = ((), (), s32[]{:S(2)}) async-start(), calls=%async_computation.1 | async-start | bytes 8912896 | tf_op jit(solution)/shard_map/all_gather | solution.py:11
  33.7 14.5 %copy-start.1 = (bf16[8,64,4096]{2,1,0:T(8,128)(2,1)S(1)}, bf16[8,64,4096]{2,1,0:T(8,128)(2,1)}, u32[]{:S(2)}) copy-start(bf16[8,64,4096]{2,1,0:T(8,128)(2,1)} %param.5) | copy-start | bytes 12582916
  65.1 197.6 %all-gather.11.cloned.1.call-start = ((), (), s32[]{:S(2)}) async-start(), calls=%async_computation.2 | async-start | bytes 8912896 | tf_op jit(solution)/shard_map/all_gather | solution.py:11
  154.6 26.3 %collective-permute-start = (f32[64,4096]{1,0:T(8,128)S(1)}, f32[64,4096]{1,0:T(8,128)S(1)}, u32[]{:S(2)}, u32[]{:S(2)}) collective-permute-start(f32[64,4096]{1,0:T(8,128)S(1)} %fusion.3), channel_id=1, source_target_pairs={{112,0},{0,16},{16,32},{32,48},{48,64},{64,80},{80,96},{96,112},{1... | collective-permute-start | bytes 3145736 | tf_op jit(solution)/shard_map/ppermute | solution.py:19
  192.6 192.0 %all-gather.13.cloned.1.call-start = ((), (), s32[]{:S(2)}) async-start(), calls=%async_computation.3 | async-start | bytes 8912896 | tf_op jit(solution)/shard_map/all_gather | solution.py:11
  276.5 26.3 %collective-permute-start.1 = (f32[64,4096]{1,0:T(8,128)S(1)}, f32[64,4096]{1,0:T(8,128)S(1)}, u32[]{:S(2)}, u32[]{:S(2)}) collective-permute-start(f32[64,4096]{1,0:T(8,128)S(1)} %fusion.2), channel_id=1, source_target_pairs={{112,0},{0,16},{16,32},{32,48},{48,64},{64,80},{80,96},{96,112},{1... | collective-permute-start | bytes 3145736 | tf_op jit(solution)/shard_map/ppermute | solution.py:19
  314.6 192.0 %all-gather.15.cloned.1.call-start = ((), (), s32[]{:S(2)}) async-start(), calls=%async_computation.4 | async-start | bytes 8912896 | tf_op jit(solution)/shard_map/all_gather | solution.py:11
  398.5 26.3 %collective-permute-start.2 = (f32[64,4096]{1,0:T(8,128)S(1)}, f32[64,4096]{1,0:T(8,128)S(1)}, u32[]{:S(2)}, u32[]{:S(2)}) collective-permute-start(f32[64,4096]{1,0:T(8,128)S(1)} %fusion.1), channel_id=1, source_target_pairs={{112,0},{0,16},{16,32},{32,48},{48,64},{64,80},{80,96},{96,112},{1... | collective-permute-start | bytes 3145736 | tf_op jit(solution)/shard_map/ppermute | solution.py:19
  436.6 268.5 %all-reduce.2.cloned.1.call-start = ((), (), s32[]{:S(2)}) async-start(), calls=%async_computation | async-start | bytes 8388608 | tf_op jit(solution)/shard_map/psum | solution.py:57
Sparse Core Ops, SparseCore 0:
  65.2 74.9 all-gather.8
  192.7 69.8 all-gather.10
  314.7 69.8 all-gather.12
  436.7 69.8 all-gather.14
  523.8 181.2 all-reduce.1
